TPU v7x, 32 devices: a whole 2x2x4 slice. The times are simulated.
32 devices in a mesh: passage: 2 (over x), brick: 16 (over z, y, core).
Axes of the slice: x: 2, y: 2, z: 4, core: 2. Of those that a mesh axis runs over, the one named last changes fastest.
Arguments:
- jac_blocks: bfloat16 [2, 25, 16, 8192], P('passage', None, None, 'brick'), may hold values from -6 to 6
- psi_start: float32 [2, 10, 16, 64, 128], P('passage', None, 'brick'), may hold values from -6 to 6
- source: float32 [2, 10, 16, 64, 128], P('passage', None, 'brick'), may hold values from -6 to 6
- pseudo_step: float32 [2, 16, 64, 128], P('passage', 'brick'), may hold values from 0.1 to 0.4
- dissipation: float32 [2, 16, 64, 128], P('passage', 'brick'), may hold values from 0.04 to 0.15
- freq_volume: float32 [2, 16, 64, 128], P('passage', 'brick'), may hold values from 0.2 to 2
- normals: float32 [2, 3, 16, 64], P('passage', None, 'brick'), may hold values from -6 to 6
- face_owner: int32 [2, 1024, 1], P('passage', 'brick'), may hold values from 0 to 15; in each aligned block of 64 rows (0 to 63, 64 to 127, ..., all dimensions but the last counted through in order) at most 16 rows name the same one
- face_slot: int32 [2, 1024], P('passage', 'brick'), may hold values from 0 to 255
Outputs:
- adjoint: float32 [2, 10, 16, 64, 128], P('passage', None, 'brick')
- sensitivity: float32 [2, 6, 4096], P('passage', None, 'brick')
Inputs may be any that keep to these rules, and one draw needn't show every extreme that they name: `face_owner`: in the 64 faces of one device (aligned blocks of the rows), no brick is named by more than 16 faces, and in some block some brick is named by exactly 16.
All inputs are finite; a program needn't handle non-finite values.
Results may differ from a plain program's by a relative error of at most 0.0003.
Values may be sent and summed in bfloat16 or wider, within the bound.
A program may use at most 64 MiB of HBM per device.

v0:
```python
import math
import jax
import jax.numpy as jnp
from jax import lax
from jax.sharding import PartitionSpec as P

NODE_DEV = 256
SWEEPS = 2
ND = 1
BLADES = 36


def padded(value, sides, width, wrap):
    for axis, dim in sides:
        peers, length = (lax.axis_size(axis), value.shape[dim])
        up = [(i, (i + 1) % peers) for i in range(peers if wrap else peers - 1)]
        down = [(j, i) for i, j in up]
        last = lax.slice_in_dim(value, length - width, length, axis=dim)
        initial = lax.slice_in_dim(value, 0, width, axis=dim)
        before = lax.ppermute(last, axis, up)
        after = lax.ppermute(initial, axis, down)
        value = jnp.concatenate([before, value, after], axis=dim)
    return value


def rotate(rim, turn):
    cosine = math.cos(turn)
    sine = math.sin(turn)
    real_part = rim[:, :5]
    imag_part = rim[:, 5:]
    return jnp.concatenate(
        [real_part * cosine - imag_part * sine, real_part * sine + imag_part * cosine], axis=1
    )


def transpose_apply(tiles, diff):
    total_real = jnp.zeros_like(diff[:, :5])
    total_imag = jnp.zeros_like(diff[:, :5])
    for row_index in range(5):
        column = tiles[:, row_index * 5 : row_index * 5 + 5].astype(jnp.float32)
        total_real = total_real + column * diff[:, row_index : row_index + 1]
        total_imag = total_imag + column * diff[:, 5 + row_index : 6 + row_index]
    return jnp.concatenate([total_real, total_imag], axis=1)


def advance(
    state,
    source,
    pseudo_step,
    dissipation,
    freq_volume,
    convect_fn,
    cycle_index,
    passes,
    phase_angle,
):
    padded_i = padded(state, (("brick", 2),), 1, False)
    padded_j = padded(state.astype(jnp.bfloat16), (("passage", 3),), 1, True).astype(state.dtype)
    below_rim = padded_j[:, :, :, :1]
    above_rim = padded_j[:, :, :, -1:]
    below_rim = jnp.where(cycle_index == 0, rotate(below_rim, -phase_angle), below_rim)
    above_rim = jnp.where(cycle_index == passes - 1, rotate(above_rim, phase_angle), above_rim)
    fixed_j = jnp.concatenate([below_rim, state, above_rim], axis=3)
    padded_k = jnp.pad(state, ((0, 0), (0, 0), (0, 0), (0, 0), (1, 1)))
    beside = padded_i[:, :, 2:] + padded_i[:, :, :-2]
    beside = beside + fixed_j[:, :, :, 2:] + fixed_j[:, :, :, :-2]
    beside = beside + padded_k[..., 2:] + padded_k[..., :-2]
    diff = 0.5 * (padded_i[:, :, 2:] - padded_i[:, :, :-2])
    convect = convect_fn(diff)
    omega = freq_volume[:, None]
    spin = jnp.concatenate([omega * state[:, 5:], -omega * state[:, :5]], axis=1)
    resid = convect + spin + dissipation[:, None] * (6.0 * state - beside) - source
    return state - pseudo_step[:, None] * resid


def body(
    jac_blocks,
    psi_start,
    source,
    pseudo_step,
    dissipation,
    freq_volume,
    normals,
    face_owner,
    face_slot,
):
    passes = lax.axis_size("passage")
    cycle_index = lax.axis_index("passage")
    bricks = lax.axis_size("brick")
    planes = psi_start.shape[2]
    width_j = psi_start.shape[3]
    width_k = psi_start.shape[4]
    phase_angle = 2.0 * math.pi * ND * passes / BLADES
    relaid = lax.all_to_all(jac_blocks, "brick", split_axis=2, concat_axis=3, tiled=True)
    tiles = relaid.reshape(1, 25, planes, width_j, width_k)

    def convect_fn(diff):
        return transpose_apply(tiles, diff)

    state = psi_start
    for sweep in range(SWEEPS):
        state = advance(
            state,
            source,
            pseudo_step,
            dissipation,
            freq_volume,
            convect_fn,
            cycle_index,
            passes,
            phase_angle,
        )
    wall_state = state[0, :, :, :, 0]
    face_normals = normals[0]
    values = jnp.concatenate(
        [face_normals * wall_state[1:4], face_normals * wall_state[6:9]], axis=0
    )
    values = values.reshape(6, planes * width_j)
    owners = face_owner[0, :, 0]
    slots = face_slot[0]
    node_ids = owners * NODE_DEV + slots
    local_terms = jnp.zeros((6, NODE_DEV * bricks), jnp.float32).at[:, node_ids].add(values)
    summed = lax.psum_scatter(local_terms, "brick", scatter_dimension=1, tiled=True)
    sensitivity = summed[None]
    return (state, sensitivity)


def solution(mesh):
    placed = (
        P("passage", None, None, "brick"),
        P("passage", None, "brick", None, None),
        P("passage", None, "brick", None, None),
        P("passage", "brick", None, None),
        P("passage", "brick", None, None),
        P("passage", "brick", None, None),
        P("passage", None, "brick", None),
        P("passage", "brick", None),
        P("passage", "brick"),
    )
    return jax.shard_map(
        body,
        mesh=mesh,
        in_specs=placed,
        out_specs=(P("passage", None, "brick", None, None), P("passage", None, "brick")),
        check_vma=False,
    )
```

profile of v0, /device:TPU:0, one launch (start us, length us, event | category | flops | bytes accessed | tf_op | source)
XLA Modules:
  0.0 128.0 jit_solution(5724360956886795302)
XLA Ops:
  7.2 0.0 copy-start
  7.2 0.0 copy-start.3
  7.2 0.0 copy-start.7
  7.2 0.0 copy-start.8
  7.2 2.5 %collective-permute-start.1 = (f32[1,10,1,64,128]{4,3,1,2,0:T(8,128)}, f32[1,10,1,64,128]{4,3,1,2,0:T(8,128)S(1)}, u32[]{:S(2)}, u32[]{:S(2)}) collective-permute-start(f32[1,10,1,64,128]{4,3,1,2,0:T(8,128)} %bitcast.71), channel_id=1, source_target_pairs={{0,1},{1,2},{2,3},{3,4},{4,5},{5,6},{6,7},{7,8},{8,9},{9,10},{10,1... | collective-permute-start | bytes 983048 | tf_op jit(solution)/shard_map/ppermute | solution.py:20
  9.8 1.3 %collective-permute-start = (f32[1,10,1,64,128]{4,3,1,2,0:T(8,128)}, f32[1,10,1,64,128]{4,3,1,2,0:T(8,128)S(1)}, u32[]{:S(2)}, u32[]{:S(2)}) collective-permute-start(f32[1,10,1,64,128]{4,3,1,2,0:T(8,128)} %bitcast.72), channel_id=1, source_target_pairs={{1,0},{2,1},{3,2},{4,3},{5,4},{6,5},{7,6},{8,7},{9,8},{10,9},{11,1... | collective-permute-start | bytes 983048 | tf_op jit(solution)/shard_map/ppermute | solution.py:21
  11.1 1.0 bitcast_convert_fusion
  12.1 2.4 %collective-permute-start.2 = (bf16[1,10,1,1,128]{4,3,1,2,0:T(2,128)(2,1)S(1)}, bf16[1,10,1,1,128]{4,3,1,2,0:T(2,128)(2,1)S(1)}, u32[]{:S(2)}, u32[]{:S(2)}) collective-permute-start(bf16[1,10,1,1,128]{4,3,1,2,0:T(2,128)(2,1)S(1)} %get-tuple-element.64), channel_id=1, source_target_pairs={{0,16},{16,0},{1,17},{17,1},{2,18},{18,2},{3,19},{19,3},{4,20},{20... | collective-permute-start | bytes 7688 | tf_op jit(solution)/shard_map/ppermute | solution.py:20
  14.5 0.1 collective-permute-start.3
  14.5 2.0 %copy.66 = bf16[1,25,16,512]{3,1,0,2:T(8,128)(2,1)} copy(bf16[1,25,16,512]{3,2,1,0:T(8,128)(2,1)} %param.9) | data formatting | bytes 819200 | tf_op args[0]
  16.6 8.9 %all-to-all-start = ((bf16[1,25,16,512]{3,1,0,2:T(8,128)(2,1)}), bf16[1,25,16,512]{3,1,0,2:T(8,128)(2,1)S(1)}, u32[]{:S(2)}, u32[]{:S(2)}) async-start(bf16[1,25,16,512]{3,1,0,2:T(8,128)(2,1)} %copy.66), calls=%async_computation | async-start | bytes 1048576 | tf_op jit(solution)/shard_map/all_to_all | solution.py:94
  25.5 0.0 reduce-scatter.2.cloned.1.call-start
  25.6 0.0 copy-done.3
  25.6 0.0 copy-done
  25.6 0.0 copy-done.7
  25.6 0.0 copy-done.8
  25.7 0.0 collective-permute-done.2
  25.7 0.0 collective-permute-done.3
  25.8 0.0 collective-permute-done.1
  25.8 0.0 collective-permute-done
  25.8 0.0 copy-start.1
  25.8 0.0 copy-start.4
  25.9 0.0 copy-start.5
  25.9 13.9 %all-to-all-done = bf16[1,25,16,512]{3,1,0,2:T(8,128)(2,1)S(1)} async-done(((bf16[1,25,16,512]{3,1,0,2:T(8,128)(2,1)}), bf16[1,25,16,512]{3,1,0,2:T(8,128)(2,1)S(1)}, u32[]{:S(2)}, u32[]{:S(2)}) %all-to-all-start) | async-done | bytes 409632 | tf_op jit(solution)/shard_map/all_to_all | solution.py:94
  39.8 0.2 copy.67
  40.0 0.2 reshape.329
  40.3 0.1 fusion.29
  40.4 0.1 fusion.25
  40.5 0.0 copy-done.1
  40.5 0.0 copy-done.4
  40.5 0.0 copy-done.5
  40.5 0.3 fusion.50
  40.8 1.6 %collective-permute-start.6 = (bf16[1,10,1,1,128]{4,3,1,2,0:T(2,128)(2,1)S(1)}, bf16[1,10,1,1,128]{4,3,1,2,0:T(2,128)(2,1)S(1)}, u32[]{:S(2)}, u32[]{:S(2)}) collective-permute-start(bf16[1,10,1,1,128]{4,3,1,2,0:T(2,128)(2,1)S(1)} %get-tuple-element.62), channel_id=1, source_target_pairs={{0,16},{16,0},{1,17},{17,1},{2,18},{18,2},{3,19},{19,3},{4,20},{20... | collective-permute-start | bytes 7688 | tf_op jit(solution)/shard_map/ppermute | solution.py:20
  42.4 0.5 collective-permute-start.7
  42.9 1.5 %collective-permute-start.5 = (f32[1,10,1,64,128]{4,3,1,2,0:T(8,128)S(1)}, f32[1,10,1,64,128]{4,3,1,2,0:T(8,128)S(1)}, u32[]{:S(2)}, u32[]{:S(2)}) collective-permute-start(f32[1,10,1,64,128]{4,3,1,2,0:T(8,128)S(1)} %get-tuple-element.21), channel_id=1, source_target_pairs={{0,1},{1,2},{2,3},{3,4},{4,5},{5,6},{6,7},{7,8},{8,9},{9,10},{10,1... | collective-permute-start | bytes 983048 | tf_op jit(solution)/shard_map/ppermute | solution.py:20
  44.5 1.3 %collective-permute-start.4 = (f32[1,10,1,64,128]{4,3,1,2,0:T(8,128)S(1)}, f32[1,10,1,64,128]{4,3,1,2,0:T(8,128)S(1)}, u32[]{:S(2)}, u32[]{:S(2)}) collective-permute-start(f32[1,10,1,64,128]{4,3,1,2,0:T(8,128)S(1)} %get-tuple-element.21), channel_id=1, source_target_pairs={{1,0},{2,1},{3,2},{4,3},{5,4},{6,5},{7,6},{8,7},{9,8},{10,9},{11,1... | collective-permute-start | bytes 983048 | tf_op jit(solution)/shard_map/ppermute | solution.py:21
  45.8 0.0 collective-permute-done.6
  45.8 0.2 collective-permute-done.7
  46.1 0.0 collective-permute-done.5
  46.1 2.3 %collective-permute-done.4 = f32[1,10,1,64,128]{4,3,1,2,0:T(8,128)S(1)} collective-permute-done((f32[1,10,1,64,128]{4,3,1,2,0:T(8,128)S(1)}, f32[1,10,1,64,128]{4,3,1,2,0:T(8,128)S(1)}, u32[]{:S(2)}, u32[]{:S(2)}) %collective-permute-start.4) | collective-permute-done | bytes 327712 | tf_op jit(solution)/shard_map/ppermute | solution.py:21
  48.5 0.0 copy-start.6
  48.5 0.1 fusion.33
  48.6 0.1 fusion.37
  48.7 0.4 fusion.17
  49.1 0.0 copy-start.2
  49.1 0.1 slice_reduce_fusion.1
  49.2 0.0 copy-done.6
  49.3 0.1 copy.84
  49.4 2.2 %scatter_custom_fusion = f32[6,4096]{0,1:T(8,128)} fusion(s32[64]{0:T(128)S(1)} %fusion.49, f32[]{:T(128)} %constant.11.clone.1, f32[6,1,64]{0,2,1:T(8,128)S(1)} %copy.84), kind=kCustom, calls=%fused_computation.1 | custom fusion | flops 384 | bytes 131076 | tf_op jit(solution)/shard_map/scatter-add | solution.py:122
  51.6 0.0 reduce-scatter.2.cloned.1.call-update
  51.6 0.0 copy-done.2
  51.6 68.0 %reduce-scatter.2.cloned.1.call-done = f32[6,256]{0,1:T(8,128)} async-done(((f32[6,4096]{0,1:T(8,128)}), f32[6,256]{0,1:T(8,128)}) %reduce-scatter.2.cloned.1.call-update) | async-done | bytes 6160 | tf_op jit(solution)/shard_map/reduce_scatter | solution.py:123
  119.6 1.6 %copy.82 = f32[1,6,256]{2,0,1:T(1,128)} copy(f32[1,6,256]{1,2,0:T(8,128)} %bitcast.82) | data formatting | bytes 12288
  (19 shorter events, 0.4 us)
Async XLA Ops:
  7.2 18.4 %copy-start = (f32[1,10,1,64,128]{4,3,2,1,0:T(8,128)S(1)}, f32[1,10,1,64,128]{4,3,2,1,0:T(8,128)}, u32[]{:S(2)}) copy-start(f32[1,10,1,64,128]{4,3,2,1,0:T(8,128)} %param.10) | copy-start | bytes 983044
  7.2 18.4 %copy-start.3 = (f32[1,1,64,128]{3,2,1,0:T(8,128)S(1)}, f32[1,1,64,128]{3,2,1,0:T(8,128)}, u32[]{:S(2)}) copy-start(f32[1,1,64,128]{3,2,1,0:T(8,128)} %param.14) | copy-start | bytes 98308
  7.2 18.4 %copy-start.7 = (s32[1,64]{1,0:T(1,128)S(1)}, s32[1,64]{1,0:T(1,128)}, u32[]{:S(2)}) copy-start(s32[1,64]{1,0:T(1,128)} %param.17) | copy-start | bytes 772
  7.2 18.4 %copy-start.8 = (s32[1,64,1]{1,2,0:T(1,128)S(1)}, s32[1,64,1]{1,2,0:T(1,128)}, u32[]{:S(2)}) copy-start(s32[1,64,1]{1,2,0:T(1,128)} %param.16) | copy-start | bytes 772
  7.2 18.6 %collective-permute-start.1 = (f32[1,10,1,64,128]{4,3,1,2,0:T(8,128)}, f32[1,10,1,64,128]{4,3,1,2,0:T(8,128)S(1)}, u32[]{:S(2)}, u32[]{:S(2)}) collective-permute-start(f32[1,10,1,64,128]{4,3,1,2,0:T(8,128)} %bitcast.71), channel_id=1, source_target_pairs={{0,1},{1,2},{2,3},{3,4},{4,5},{5,6},{6,7},{7,8},{8,9},{9,10},{10,1... | collective-permute-start | bytes 983048 | tf_op jit(solution)/shard_map/ppermute | solution.py:20
  9.8 16.0 %collective-permute-start = (f32[1,10,1,64,128]{4,3,1,2,0:T(8,128)}, f32[1,10,1,64,128]{4,3,1,2,0:T(8,128)S(1)}, u32[]{:S(2)}, u32[]{:S(2)}) collective-permute-start(f32[1,10,1,64,128]{4,3,1,2,0:T(8,128)} %bitcast.72), channel_id=1, source_target_pairs={{1,0},{2,1},{3,2},{4,3},{5,4},{6,5},{7,6},{8,7},{9,8},{10,9},{11,1... | collective-permute-start | bytes 983048 | tf_op jit(solution)/shard_map/ppermute | solution.py:21
  12.1 13.6 %collective-permute-start.2 = (bf16[1,10,1,1,128]{4,3,1,2,0:T(2,128)(2,1)S(1)}, bf16[1,10,1,1,128]{4,3,1,2,0:T(2,128)(2,1)S(1)}, u32[]{:S(2)}, u32[]{:S(2)}) collective-permute-start(bf16[1,10,1,1,128]{4,3,1,2,0:T(2,128)(2,1)S(1)} %get-tuple-element.64), channel_id=1, source_target_pairs={{0,16},{16,0},{1,17},{17,1},{2,18},{18,2},{3,19},{19,3},{4,20},{20... | collective-permute-start | bytes 7688 | tf_op jit(solution)/shard_map/ppermute | solution.py:20
  14.5 11.2 %collective-permute-start.3 = (bf16[1,10,1,1,128]{4,3,1,2,0:T(2,128)(2,1)S(1)}, bf16[1,10,1,1,128]{4,3,1,2,0:T(2,128)(2,1)S(1)}, u32[]{:S(2)}, u32[]{:S(2)}) collective-permute-start(bf16[1,10,1,1,128]{4,3,1,2,0:T(2,128)(2,1)S(1)} %get-tuple-element.65), channel_id=1, source_target_pairs={{16,0},{0,16},{17,1},{1,17},{18,2},{2,18},{19,3},{3,19},{20,4},{4,... | collective-permute-start | bytes 7688 | tf_op jit(solution)/shard_map/ppermute | solution.py:21
  16.6 23.2 %all-to-all-start = ((bf16[1,25,16,512]{3,1,0,2:T(8,128)(2,1)}), bf16[1,25,16,512]{3,1,0,2:T(8,128)(2,1)S(1)}, u32[]{:S(2)}, u32[]{:S(2)}) async-start(bf16[1,25,16,512]{3,1,0,2:T(8,128)(2,1)} %copy.66), calls=%async_computation | async-start | bytes 1048576 | tf_op jit(solution)/shard_map/all_to_all | solution.py:94
  25.5 94.1 %reduce-scatter.2.cloned.1.call-start = ((), (), s32[]{:S(2)}) async-start(), calls=%async_computation.2 | async-start | bytes 2228224 | tf_op jit(solution)/shard_map/reduce_scatter | solution.py:123
  25.8 14.6 %copy-start.1 = (f32[1,10,1,64,128]{4,3,2,1,0:T(8,128)S(1)}, f32[1,10,1,64,128]{4,3,2,1,0:T(8,128)}, u32[]{:S(2)}) copy-start(f32[1,10,1,64,128]{4,3,2,1,0:T(8,128)} %param.11) | copy-start | bytes 983044
  25.8 14.6 %copy-start.4 = (f32[1,1,64,128]{3,2,1,0:T(8,128)S(1)}, f32[1,1,64,128]{3,2,1,0:T(8,128)}, u32[]{:S(2)}) copy-start(f32[1,1,64,128]{3,2,1,0:T(8,128)} %param.13) | copy-start | bytes 98308
  25.9 14.6 %copy-start.5 = (f32[1,1,64,128]{3,2,1,0:T(8,128)S(1)}, f32[1,1,64,128]{3,2,1,0:T(8,128)}, u32[]{:S(2)}) copy-start(f32[1,1,64,128]{3,2,1,0:T(8,128)} %param.12) | copy-start | bytes 98308
  40.8 4.9 %collective-permute-start.6 = (bf16[1,10,1,1,128]{4,3,1,2,0:T(2,128)(2,1)S(1)}, bf16[1,10,1,1,128]{4,3,1,2,0:T(2,128)(2,1)S(1)}, u32[]{:S(2)}, u32[]{:S(2)}) collective-permute-start(bf16[1,10,1,1,128]{4,3,1,2,0:T(2,128)(2,1)S(1)} %get-tuple-element.62), channel_id=1, source_target_pairs={{0,16},{16,0},{1,17},{17,1},{2,18},{18,2},{3,19},{19,3},{4,20},{20... | collective-permute-start | bytes 7688 | tf_op jit(solution)/shard_map/ppermute | solution.py:20
  42.4 3.6 %collective-permute-start.7 = (bf16[1,10,1,1,128]{4,3,1,2,0:T(2,128)(2,1)S(1)}, bf16[1,10,1,1,128]{4,3,1,2,0:T(2,128)(2,1)S(1)}, u32[]{:S(2)}, u32[]{:S(2)}) collective-permute-start(bf16[1,10,1,1,128]{4,3,1,2,0:T(2,128)(2,1)S(1)} %get-tuple-element.63), channel_id=1, source_target_pairs={{16,0},{0,16},{17,1},{1,17},{18,2},{2,18},{19,3},{3,19},{20,4},{4,... | collective-permute-start | bytes 7688 | tf_op jit(solution)/shard_map/ppermute | solution.py:21
  42.9 3.1 %collective-permute-start.5 = (f32[1,10,1,64,128]{4,3,1,2,0:T(8,128)S(1)}, f32[1,10,1,64,128]{4,3,1,2,0:T(8,128)S(1)}, u32[]{:S(2)}, u32[]{:S(2)}) collective-permute-start(f32[1,10,1,64,128]{4,3,1,2,0:T(8,128)S(1)} %get-tuple-element.21), channel_id=1, source_target_pairs={{0,1},{1,2},{2,3},{3,4},{4,5},{5,6},{6,7},{7,8},{8,9},{9,10},{10,1... | collective-permute-start | bytes 983048 | tf_op jit(solution)/shard_map/ppermute | solution.py:20
  44.5 4.0 %collective-permute-start.4 = (f32[1,10,1,64,128]{4,3,1,2,0:T(8,128)S(1)}, f32[1,10,1,64,128]{4,3,1,2,0:T(8,128)S(1)}, u32[]{:S(2)}, u32[]{:S(2)}) collective-permute-start(f32[1,10,1,64,128]{4,3,1,2,0:T(8,128)S(1)} %get-tuple-element.21), channel_id=1, source_target_pairs={{1,0},{2,1},{3,2},{4,3},{5,4},{6,5},{7,6},{8,7},{9,8},{10,9},{11,1... | collective-permute-start | bytes 983048 | tf_op jit(solution)/shard_map/ppermute | solution.py:21
  48.5 0.7 copy-start.6
  49.1 2.5 %copy-start.2 = (f32[1,10,1,64,128]{4,3,1,2,0:T(8,128)}, f32[1,10,1,64,128]{4,3,1,2,0:T(8,128)S(1)}, u32[]{:S(2)}) copy-start(f32[1,10,1,64,128]{4,3,1,2,0:T(8,128)S(1)} %fusion.17) | copy-start | bytes 983044
Sparse Core Ops, SparseCore 0:
  51.7 67.8 reduce-scatter.1
where the time goes:
time: 128 us
  waiting for transfers between devices  84.5 us (66%)
  starting transfers between devices  20.1 us (16%)
  between operations  14.5 us (11%)
  other arithmetic  4.52 us (4%)
  local copies, waits for them, and re-layouts  4.46 us (3%)
    reduce_scatter x1, waiting for transfers between devices, body(): lax.psum_scatter(local_terms, 'brick', scatter_dimension=1, tiled=True)  68 us
    all_to_all x1, waiting for transfers between devices, body(): lax.all_to_all(jac_blocks, 'brick', split_axis=2, concat_axis=3, tiled=True)  13.9 us
    all_to_all x1, starting transfers between devices, body(): lax.all_to_all(jac_blocks, 'brick', split_axis=2, concat_axis=3, tiled=True)  8.92 us
    ppermute x4, starting transfers between devices, padded(): before = lax.ppermute(last, axis, up)  7.99 us
    unnamed x20, local copies, waits for them, and re-layouts  3.67 us
    ppermute x4, starting transfers between devices, padded(): after = lax.ppermute(initial, axis, down)  3.2 us
    ppermute x4, waiting for transfers between devices, padded(): after = lax.ppermute(initial, axis, down)  2.58 us
  transfers between devices with their start and end apart: 10, of which 4 were waited for; matrix products, arithmetic and copies ran while one was open for 3% of the time, Pallas kernels for 0%

commit v1 on v0

--- a/solution.py
+++ b/solution.py
@@ -91,7 +91,18 @@
     width_j = psi_start.shape[3]
     width_k = psi_start.shape[4]
     phase_angle = 2.0 * math.pi * ND * passes / BLADES
-    relaid = lax.all_to_all(jac_blocks, "brick", split_axis=2, concat_axis=3, tiled=True)
+    ways, here = (lax.axis_size("brick"), lax.axis_index("brick"))
+    width_2 = jac_blocks.shape[2] // ways
+    shape = list(jac_blocks.shape)
+    shape[2] = width_2
+    height = shape[3]
+    shape[3] = height * ways
+    relaid = jnp.zeros(shape, jac_blocks.dtype)
+    for mask in range(ways):
+        part = lax.dynamic_slice_in_dim(jac_blocks, (here ^ mask) * width_2, width_2, axis=2)
+        if mask:
+            part = lax.ppermute(part, "brick", [(d, d ^ mask) for d in range(ways)])
+        relaid = lax.dynamic_update_slice_in_dim(relaid, part, (here ^ mask) * height, axis=3)
     tiles = relaid.reshape(1, 25, planes, width_j, width_k)
 
     def convect_fn(diff):

time: 128 us -> 141 us (1.10)
  starting transfers between devices: 20.1 us -> 41.7 us
  waiting for transfers between devices: 84.5 us -> 73.1 us
  local copies, waits for them, and re-layouts: 4.46 us -> 7 us
    ppermute x0 -> x15, starting transfers between devices: none -> 28.7 us  [body(): part = lax.ppermute(part, 'brick', [(d, d ^ mask) for d in range(ways)])]
    all_to_all x1 -> x0, waiting for transfers between devices: 13.9 us -> none  [body(): lax.all_to_all(jac_blocks, 'brick', split_axis=2, concat_axis=3, tiled=True)]
    all_to_all x1 -> x0, starting transfers between devices: 8.92 us -> none  [body(): lax.all_to_all(jac_blocks, 'brick', split_axis=2, concat_axis=3, tiled=True)]
    ppermute x0 -> x15, waiting for transfers between devices: none -> 6.91 us  [body(): part = lax.ppermute(part, 'brick', [(d, d ^ mask) for d in range(ways)])]
    reduce_scatter x1, waiting for transfers between devices: 68 us -> 61.9 us  [body(): lax.psum_scatter(local_terms, 'brick', scatter_dimension=1, tiled=True)]
    dynamic_slice x0 -> x1, local copies, waits for them, and re-layouts: none -> 4.14 us  [body(): lax.dynamic_slice_in_dim(jac_blocks, (here ^ mask) * width_2, width_2, ax...]
    ppermute x4, waiting for transfers between devices: 0.01 us -> 2.91 us  [padded(): before = lax.ppermute(last, axis, up)]
  transfers between devices with their start and end apart: 10 -> 24, of which waited for: 4 -> 10; matrix products, arithmetic and copies ran while one was open for 3% -> 4% of each run, Pallas kernels for 0% -> 0%
where the time goes in v1:
time: 141 us
  waiting for transfers between devices  73.1 us (52%)
  starting transfers between devices  41.7 us (30%)
  between operations  14.8 us (10%)
  local copies, waits for them, and re-layouts  7 us (5%)
  other arithmetic  4.54 us (3%)
    reduce_scatter x1, waiting for transfers between devices, body(): lax.psum_scatter(local_terms, 'brick', scatter_dimension=1, tiled=True)  61.9 us
    ppermute x15, starting transfers between devices, body(): part = lax.ppermute(part, 'brick', [(d, d ^ mask) for d in range(ways)])  28.7 us
    ppermute x4, starting transfers between devices, padded(): before = lax.ppermute(last, axis, up)  9.17 us
    ppermute x15, waiting for transfers between devices, body(): part = lax.ppermute(part, 'brick', [(d, d ^ mask) for d in range(ways)])  6.91 us
    dynamic_slice x1, local copies, waits for them, and re-layouts, body(): lax.dynamic_slice_in_dim(jac_blocks, (here ^ mask) * width_2, width_2, ax...  4.14 us
    ppermute x4, starting transfers between devices, padded(): after = lax.ppermute(initial, axis, down)  3.83 us
    ppermute x4, waiting for transfers between devices, padded(): before = lax.ppermute(last, axis, up)  2.91 us
  transfers between devices with their start and end apart: 24, of which 10 were waited for; matrix products, arithmetic and copies ran while one was open for 4% of the time, Pallas kernels for 0%

profile of v1, /device:TPU:0, one launch (start us, length us, event | category | flops | bytes accessed | tf_op | source)
XLA Modules:
  0.0 141.2 jit_solution(16507652592194224478)
XLA Ops:
  7.2 0.0 copy-start
  7.2 0.0 reduce-scatter.2.cloned.1.call-start
  7.3 1.4 %collective-permute-start.15 = (f32[1,10,1,64,128]{4,3,1,2,0:T(8,128)}, f32[1,10,1,64,128]{4,3,1,2,0:T(8,128)S(1)}, u32[]{:S(2)}, u32[]{:S(2)}) collective-permute-start(f32[1,10,1,64,128]{4,3,1,2,0:T(8,128)} %bitcast.77), channel_id=1, source_target_pairs={{1,0},{2,1},{3,2},{4,3},{5,4},{6,5},{7,6},{8,7},{9,8},{10,9},{11,1... | collective-permute-start | bytes 983048 | tf_op jit(solution)/shard_map/ppermute | solution.py:21
  8.7 3.1 %collective-permute-start.16 = (f32[1,10,1,64,128]{4,3,1,2,0:T(8,128)}, f32[1,10,1,64,128]{4,3,1,2,0:T(8,128)S(1)}, u32[]{:S(2)}, u32[]{:S(2)}) collective-permute-start(f32[1,10,1,64,128]{4,3,1,2,0:T(8,128)} %bitcast.78), channel_id=1, source_target_pairs={{0,1},{1,2},{2,3},{3,4},{4,5},{5,6},{6,7},{7,8},{8,9},{9,10},{10,1... | collective-permute-start | bytes 983048 | tf_op jit(solution)/shard_map/ppermute | solution.py:20
  11.9 4.1 %constant_dynamic-slice_fusion = (bf16[1,25,1,512]{3,2,1,0:T(2,128)(2,1)S(1)}, bf16[1,25,1,512]{3,2,1,0:T(2,128)(2,1)S(1)}, bf16[1,25,1,512]{3,2,1,0:T(2,128)(2,...) fusion(bf16[1,25,16,512]{3,2,1,0:T(8,128)(2,1)} %param.9, ...), kind=kLoop, calls=%fused_computation.119 | loop fusion | bytes 819264 | tf_op jit(solution)/shard_map/dynamic_slice | solution.py:102
  16.0 2.7 %collective-permute-start = (bf16[1,25,1,512]{3,2,1,0:T(2,128)(2,1)S(1)}, bf16[1,25,1,512]{3,2,1,0:T(2,128)(2,1)S(1)}, u32[]{:S(2)}, u32[]{:S(2)}) collective-permute-start(bf16[1,25,1,512]{3,2,1,0:T(2,128)(2,1)S(1)} %get-tuple-element.39), channel_id=1, source_target_pairs={{0,1},{1,0},{2,3},{3,2},{4,5},{5,4},{6,7},{7,6},{8,9},{9,8},{10,11... | collective-permute-start | bytes 76808 | tf_op jit(solution)/shard_map/ppermute | solution.py:104
  18.7 1.0 bitcast_convert_fusion
  19.7 1.6 %collective-permute-start.17 = (bf16[1,10,1,1,128]{4,3,1,2,0:T(2,128)(2,1)S(1)}, bf16[1,10,1,1,128]{4,3,1,2,0:T(2,128)(2,1)S(1)}, u32[]{:S(2)}, u32[]{:S(2)}) collective-permute-start(bf16[1,10,1,1,128]{4,3,1,2,0:T(2,128)(2,1)S(1)} %get-tuple-element.78), channel_id=1, source_target_pairs={{0,16},{16,0},{1,17},{17,1},{2,18},{18,2},{3,19},{19,3},{4,20},{20... | collective-permute-start | bytes 7688 | tf_op jit(solution)/shard_map/ppermute | solution.py:20
  21.3 0.5 collective-permute-start.18
  22.1 1.3 collective-permute-done.17
  23.4 2.4 %collective-permute-start.1 = (bf16[1,25,1,512]{3,2,1,0:T(2,128)(2,1)S(1)}, bf16[1,25,1,512]{3,2,1,0:T(2,128)(2,1)S(1)}, u32[]{:S(2)}, u32[]{:S(2)}) collective-permute-start(bf16[1,25,1,512]{3,2,1,0:T(2,128)(2,1)S(1)} %get-tuple-element.38), channel_id=1, source_target_pairs={{0,2},{1,3},{2,0},{3,1},{4,6},{5,7},{6,4},{7,5},{8,10},{9,11},{10,... | collective-permute-start | bytes 76808 | tf_op jit(solution)/shard_map/ppermute | solution.py:104
  25.7 0.0 collective-permute-done.18
  25.7 0.0 collective-permute-start.2
  25.8 0.0 collective-permute-done
  25.8 1.6 %collective-permute-start.3 = (bf16[1,25,1,512]{3,2,1,0:T(2,128)(2,1)S(1)}, bf16[1,25,1,512]{3,2,1,0:T(2,128)(2,1)S(1)}, u32[]{:S(2)}, u32[]{:S(2)}) collective-permute-start(bf16[1,25,1,512]{3,2,1,0:T(2,128)(2,1)S(1)} %get-tuple-element.36), channel_id=1, source_target_pairs={{0,4},{1,5},{2,6},{3,7},{4,0},{5,1},{6,2},{7,3},{8,12},{9,13},{10,... | collective-permute-start | bytes 76808 | tf_op jit(solution)/shard_map/ppermute | solution.py:104
  27.5 0.3 collective-permute-done.1
  27.8 1.1 collective-permute-start.4
  28.9 0.8 collective-permute-done.2
  29.8 2.2 %collective-permute-start.5 = (bf16[1,25,1,512]{3,2,1,0:T(2,128)(2,1)S(1)}, bf16[1,25,1,512]{3,2,1,0:T(2,128)(2,1)S(1)}, u32[]{:S(2)}, u32[]{:S(2)}) collective-permute-start(bf16[1,25,1,512]{3,2,1,0:T(2,128)(2,1)S(1)} %get-tuple-element.34), channel_id=1, source_target_pairs={{0,6},{1,7},{2,4},{3,5},{4,2},{5,3},{6,0},{7,1},{8,14},{9,15},{10,... | collective-permute-start | bytes 76808 | tf_op jit(solution)/shard_map/ppermute | solution.py:104
  32.0 0.3 collective-permute-start.6
  32.3 2.7 %collective-permute-start.7 = (bf16[1,25,1,512]{3,2,1,0:T(2,128)(2,1)S(1)}, bf16[1,25,1,512]{3,2,1,0:T(2,128)(2,1)S(1)}, u32[]{:S(2)}, u32[]{:S(2)}) collective-permute-start(bf16[1,25,1,512]{3,2,1,0:T(2,128)(2,1)S(1)} %get-tuple-element.32), channel_id=1, source_target_pairs={{0,8},{1,9},{2,10},{3,11},{4,12},{5,13},{6,14},{7,15},{8,0},{9,1},... | collective-permute-start | bytes 76808 | tf_op jit(solution)/shard_map/ppermute | solution.py:104
  35.0 0.0 collective-permute-done.5
  35.0 1.0 collective-permute-start.8
  36.0 0.7 collective-permute-done.6
  36.7 2.1 %collective-permute-start.9 = (bf16[1,25,1,512]{3,2,1,0:T(2,128)(2,1)S(1)}, bf16[1,25,1,512]{3,2,1,0:T(2,128)(2,1)S(1)}, u32[]{:S(2)}, u32[]{:S(2)}) collective-permute-start(bf16[1,25,1,512]{3,2,1,0:T(2,128)(2,1)S(1)} %get-tuple-element.30), channel_id=1, source_target_pairs={{0,10},{1,11},{2,8},{3,9},{4,14},{5,15},{6,12},{7,13},{8,2},{9,3},... | collective-permute-start | bytes 76808 | tf_op jit(solution)/shard_map/ppermute | solution.py:104
  38.7 0.0 collective-permute-done.7
  38.8 2.4 %collective-permute-start.10 = (bf16[1,25,1,512]{3,2,1,0:T(2,128)(2,1)S(1)}, bf16[1,25,1,512]{3,2,1,0:T(2,128)(2,1)S(1)}, u32[]{:S(2)}, u32[]{:S(2)}) collective-permute-start(bf16[1,25,1,512]{3,2,1,0:T(2,128)(2,1)S(1)} %get-tuple-element.29), channel_id=1, source_target_pairs={{0,11},{1,10},{2,9},{3,8},{4,15},{5,14},{6,13},{7,12},{8,3},{9,2},... | collective-permute-start | bytes 76808 | tf_op jit(solution)/shard_map/ppermute | solution.py:104
  41.2 2.1 %collective-permute-start.11 = (bf16[1,25,1,512]{3,2,1,0:T(2,128)(2,1)S(1)}, bf16[1,25,1,512]{3,2,1,0:T(2,128)(2,1)S(1)}, u32[]{:S(2)}, u32[]{:S(2)}) collective-permute-start(bf16[1,25,1,512]{3,2,1,0:T(2,128)(2,1)S(1)} %get-tuple-element.28), channel_id=1, source_target_pairs={{0,12},{1,13},{2,14},{3,15},{4,8},{5,9},{6,10},{7,11},{8,4},{9,5},... | collective-permute-start | bytes 76808 | tf_op jit(solution)/shard_map/ppermute | solution.py:104
  43.3 0.7 collective-permute-done.9
  44.0 2.5 %collective-permute-start.12 = (bf16[1,25,1,512]{3,2,1,0:T(2,128)(2,1)S(1)}, bf16[1,25,1,512]{3,2,1,0:T(2,128)(2,1)S(1)}, u32[]{:S(2)}, u32[]{:S(2)}) collective-permute-start(bf16[1,25,1,512]{3,2,1,0:T(2,128)(2,1)S(1)} %get-tuple-element.27), channel_id=1, source_target_pairs={{0,13},{1,12},{2,15},{3,14},{4,9},{5,8},{6,11},{7,10},{8,5},{9,4},... | collective-permute-start | bytes 76808 | tf_op jit(solution)/shard_map/ppermute | solution.py:104
  46.4 3.7 %collective-permute-start.13 = (bf16[1,25,1,512]{3,2,1,0:T(2,128)(2,1)S(1)}, bf16[1,25,1,512]{3,2,1,0:T(2,128)(2,1)S(1)}, u32[]{:S(2)}, u32[]{:S(2)}) collective-permute-start(bf16[1,25,1,512]{3,2,1,0:T(2,128)(2,1)S(1)} %get-tuple-element.41), channel_id=1, source_target_pairs={{0,14},{1,15},{2,12},{3,13},{4,10},{5,11},{6,8},{7,9},{8,6},{9,7},... | collective-permute-start | bytes 76808 | tf_op jit(solution)/shard_map/ppermute | solution.py:104
  50.2 0.0 collective-permute-done.11
  50.2 2.0 %collective-permute-start.14 = (bf16[1,25,1,512]{3,2,1,0:T(2,128)(2,1)S(1)}, bf16[1,25,1,512]{3,2,1,0:T(2,128)(2,1)S(1)}, u32[]{:S(2)}, u32[]{:S(2)}) collective-permute-start(bf16[1,25,1,512]{3,2,1,0:T(2,128)(2,1)S(1)} %get-tuple-element.26), channel_id=1, source_target_pairs={{0,15},{1,14},{2,13},{3,12},{4,11},{5,10},{6,9},{7,8},{8,7},{9,6},... | collective-permute-start | bytes 76808 | tf_op jit(solution)/shard_map/ppermute | solution.py:104
  52.2 0.0 collective-permute-done.12
  52.2 1.2 collective-permute-done.13
  53.4 3.2 %collective-permute-done.14 = bf16[1,25,1,512]{3,2,1,0:T(2,128)(2,1)S(1)} collective-permute-done((bf16[1,25,1,512]{3,2,1,0:T(2,128)(2,1)S(1)}, bf16[1,25,1,512]{3,2,1,0:T(2,128)(2,1)S(1)}, u32[]{:S(2)}, u32[]{:S(2)}) %collective-permute-start.14) | collective-permute-done | bytes 25632 | tf_op jit(solution)/shard_map/ppermute | solution.py:104
  56.6 0.1 copy.116
  56.8 0.0 copy-start.1
  56.8 0.0 copy-start.4
  56.8 0.0 copy-start.5
  56.8 0.0 collective-permute-done.15
  56.9 0.1 fusion.25
  57.0 0.1 fusion.29
  57.1 0.6 copy-done.1
  57.7 0.3 fusion.50
  58.1 1.3 collective-permute-start.19
  59.4 3.1 %collective-permute-start.20 = (f32[1,10,1,64,128]{4,3,1,2,0:T(8,128)S(1)}, f32[1,10,1,64,128]{4,3,1,2,0:T(8,128)S(1)}, u32[]{:S(2)}, u32[]{:S(2)}) collective-permute-start(f32[1,10,1,64,128]{4,3,1,2,0:T(8,128)S(1)} %get-tuple-element.19), channel_id=1, source_target_pairs={{0,1},{1,2},{2,3},{3,4},{4,5},{5,6},{6,7},{7,8},{8,9},{9,10},{10,1... | collective-permute-start | bytes 983048 | tf_op jit(solution)/shard_map/ppermute | solution.py:20
  62.4 1.5 %collective-permute-start.21 = (bf16[1,10,1,1,128]{4,3,1,2,0:T(2,128)(2,1)S(1)}, bf16[1,10,1,1,128]{4,3,1,2,0:T(2,128)(2,1)S(1)}, u32[]{:S(2)}, u32[]{:S(2)}) collective-permute-start(bf16[1,10,1,1,128]{4,3,1,2,0:T(2,128)(2,1)S(1)} %get-tuple-element.76), channel_id=1, source_target_pairs={{0,16},{16,0},{1,17},{17,1},{2,18},{18,2},{3,19},{19,3},{4,20},{20... | collective-permute-start | bytes 7688 | tf_op jit(solution)/shard_map/ppermute | solution.py:20
  63.9 0.6 collective-permute-start.22
  64.6 1.6 %collective-permute-done.21 = bf16[1,10,1,1,128]{4,3,1,2,0:T(2,128)(2,1)S(1)} collective-permute-done((bf16[1,10,1,1,128]{4,3,1,2,0:T(2,128)(2,1)S(1)}, bf16[1,10,1,1,128]{4,3,1,2,0:T(2,128)(2,1)S(1)}, u32[]{:S(2)}, u32[]{:S(2)}) %collective-permute-start.21) | collective-permute-done | bytes 2592 | tf_op jit(solution)/shard_map/ppermute | solution.py:20
  66.1 1.4 %collective-permute-done.22 = bf16[1,10,1,1,128]{4,3,1,2,0:T(2,128)(2,1)S(1)} collective-permute-done((bf16[1,10,1,1,128]{4,3,1,2,0:T(2,128)(2,1)S(1)}, bf16[1,10,1,1,128]{4,3,1,2,0:T(2,128)(2,1)S(1)}, u32[]{:S(2)}, u32[]{:S(2)}) %collective-permute-start.22) | collective-permute-done | bytes 2592 | tf_op jit(solution)/shard_map/ppermute | solution.py:21
  67.7 0.0 collective-permute-done.19
  67.7 0.0 collective-permute-done.20
  67.8 0.0 copy-start.6
  67.8 0.1 fusion.33
  67.9 0.1 fusion.37
  68.0 0.3 fusion.17
  68.3 0.0 copy-start.2
  68.3 0.1 slice_reduce_fusion.1
  68.5 0.1 copy.115
  68.6 2.3 %scatter_custom_fusion = f32[6,4096]{0,1:T(8,128)} fusion(s32[64]{0:T(128)S(1)} %fusion.49, f32[]{:T(128)} %constant.64.clone.1, f32[6,1,64]{0,2,1:T(8,128)S(1)} %copy.115), kind=kCustom, calls=%fused_computation.1 | custom fusion | flops 384 | bytes 131076 | tf_op jit(solution)/shard_map/scatter-add | solution.py:133
  70.8 0.0 reduce-scatter.2.cloned.1.call-update
  70.9 61.9 %reduce-scatter.2.cloned.1.call-done = f32[6,256]{0,1:T(8,128)} async-done(((f32[6,4096]{0,1:T(8,128)}), f32[6,256]{0,1:T(8,128)}) %reduce-scatter.2.cloned.1.call-update) | async-done | bytes 6160 | tf_op jit(solution)/shard_map/reduce_scatter | solution.py:134
  132.7 1.6 %copy.113 = f32[1,6,256]{2,0,1:T(1,128)} copy(f32[1,6,256]{1,2,0:T(8,128)} %bitcast.90) | data formatting | bytes 12288
  (53 shorter events, 0.6 us)
Async XLA Ops:
  7.2 14.6 %copy-start = (f32[1,10,1,64,128]{4,3,2,1,0:T(8,128)S(1)}, f32[1,10,1,64,128]{4,3,2,1,0:T(8,128)}, u32[]{:S(2)}) copy-start(f32[1,10,1,64,128]{4,3,2,1,0:T(8,128)} %param.10) | copy-start | bytes 983044
  7.2 14.6 %copy-start.3 = (f32[1,1,64,128]{3,2,1,0:T(8,128)S(1)}, f32[1,1,64,128]{3,2,1,0:T(8,128)}, u32[]{:S(2)}) copy-start(f32[1,1,64,128]{3,2,1,0:T(8,128)} %param.14) | copy-start | bytes 98308
  7.2 14.7 %copy-start.8 = (s32[1,64,1]{1,2,0:T(1,128)S(1)}, s32[1,64,1]{1,2,0:T(1,128)}, u32[]{:S(2)}) copy-start(s32[1,64,1]{1,2,0:T(1,128)} %param.16) | copy-start | bytes 772
  7.2 14.7 %copy-start.7 = (s32[1,64]{1,0:T(1,128)S(1)}, s32[1,64]{1,0:T(1,128)}, u32[]{:S(2)}) copy-start(s32[1,64]{1,0:T(1,128)} %param.17) | copy-start | bytes 772
  7.2 125.5 %reduce-scatter.2.cloned.1.call-start = ((), (), s32[]{:S(2)}) async-start(), calls=%async_computation.1 | async-start | bytes 2228224 | tf_op jit(solution)/shard_map/reduce_scatter | solution.py:134
  7.3 49.6 %collective-permute-start.15 = (f32[1,10,1,64,128]{4,3,1,2,0:T(8,128)}, f32[1,10,1,64,128]{4,3,1,2,0:T(8,128)S(1)}, u32[]{:S(2)}, u32[]{:S(2)}) collective-permute-start(f32[1,10,1,64,128]{4,3,1,2,0:T(8,128)} %bitcast.77), channel_id=1, source_target_pairs={{1,0},{2,1},{3,2},{4,3},{5,4},{6,5},{7,6},{8,7},{9,8},{10,9},{11,1... | collective-permute-start | bytes 983048 | tf_op jit(solution)/shard_map/ppermute | solution.py:21
  8.7 48.2 %collective-permute-start.16 = (f32[1,10,1,64,128]{4,3,1,2,0:T(8,128)}, f32[1,10,1,64,128]{4,3,1,2,0:T(8,128)S(1)}, u32[]{:S(2)}, u32[]{:S(2)}) collective-permute-start(f32[1,10,1,64,128]{4,3,1,2,0:T(8,128)} %bitcast.78), channel_id=1, source_target_pairs={{0,1},{1,2},{2,3},{3,4},{4,5},{5,6},{6,7},{7,8},{8,9},{9,10},{10,1... | collective-permute-start | bytes 983048 | tf_op jit(solution)/shard_map/ppermute | solution.py:20
  16.0 9.8 %collective-permute-start = (bf16[1,25,1,512]{3,2,1,0:T(2,128)(2,1)S(1)}, bf16[1,25,1,512]{3,2,1,0:T(2,128)(2,1)S(1)}, u32[]{:S(2)}, u32[]{:S(2)}) collective-permute-start(bf16[1,25,1,512]{3,2,1,0:T(2,128)(2,1)S(1)} %get-tuple-element.39), channel_id=1, source_target_pairs={{0,1},{1,0},{2,3},{3,2},{4,5},{5,4},{6,7},{7,6},{8,9},{9,8},{10,11... | collective-permute-start | bytes 76808 | tf_op jit(solution)/shard_map/ppermute | solution.py:104
  19.7 3.7 %collective-permute-start.17 = (bf16[1,10,1,1,128]{4,3,1,2,0:T(2,128)(2,1)S(1)}, bf16[1,10,1,1,128]{4,3,1,2,0:T(2,128)(2,1)S(1)}, u32[]{:S(2)}, u32[]{:S(2)}) collective-permute-start(bf16[1,10,1,1,128]{4,3,1,2,0:T(2,128)(2,1)S(1)} %get-tuple-element.78), channel_id=1, source_target_pairs={{0,16},{16,0},{1,17},{17,1},{2,18},{18,2},{3,19},{19,3},{4,20},{20... | collective-permute-start | bytes 7688 | tf_op jit(solution)/shard_map/ppermute | solution.py:20
  21.3 4.5 %collective-permute-start.18 = (bf16[1,10,1,1,128]{4,3,1,2,0:T(2,128)(2,1)S(1)}, bf16[1,10,1,1,128]{4,3,1,2,0:T(2,128)(2,1)S(1)}, u32[]{:S(2)}, u32[]{:S(2)}) collective-permute-start(bf16[1,10,1,1,128]{4,3,1,2,0:T(2,128)(2,1)S(1)} %get-tuple-element.79), channel_id=1, source_target_pairs={{16,0},{0,16},{17,1},{1,17},{18,2},{2,18},{19,3},{3,19},{20,4},{4,... | collective-permute-start | bytes 7688 | tf_op jit(solution)/shard_map/ppermute | solution.py:21
  23.4 4.4 %collective-permute-start.1 = (bf16[1,25,1,512]{3,2,1,0:T(2,128)(2,1)S(1)}, bf16[1,25,1,512]{3,2,1,0:T(2,128)(2,1)S(1)}, u32[]{:S(2)}, u32[]{:S(2)}) collective-permute-start(bf16[1,25,1,512]{3,2,1,0:T(2,128)(2,1)S(1)} %get-tuple-element.38), channel_id=1, source_target_pairs={{0,2},{1,3},{2,0},{3,1},{4,6},{5,7},{6,4},{7,5},{8,10},{9,11},{10,... | collective-permute-start | bytes 76808 | tf_op jit(solution)/shard_map/ppermute | solution.py:104
  25.7 4.0 %collective-permute-start.2 = (bf16[1,25,1,512]{3,2,1,0:T(2,128)(2,1)S(1)}, bf16[1,25,1,512]{3,2,1,0:T(2,128)(2,1)S(1)}, u32[]{:S(2)}, u32[]{:S(2)}) collective-permute-start(bf16[1,25,1,512]{3,2,1,0:T(2,128)(2,1)S(1)} %get-tuple-element.37), channel_id=1, source_target_pairs={{0,3},{1,2},{2,1},{3,0},{4,7},{5,6},{6,5},{7,4},{8,11},{9,10},{10,... | collective-permute-start | bytes 76808 | tf_op jit(solution)/shard_map/ppermute | solution.py:104
  25.8 6.1 %collective-permute-start.3 = (bf16[1,25,1,512]{3,2,1,0:T(2,128)(2,1)S(1)}, bf16[1,25,1,512]{3,2,1,0:T(2,128)(2,1)S(1)}, u32[]{:S(2)}, u32[]{:S(2)}) collective-permute-start(bf16[1,25,1,512]{3,2,1,0:T(2,128)(2,1)S(1)} %get-tuple-element.36), channel_id=1, source_target_pairs={{0,4},{1,5},{2,6},{3,7},{4,0},{5,1},{6,2},{7,3},{8,12},{9,13},{10,... | collective-permute-start | bytes 76808 | tf_op jit(solution)/shard_map/ppermute | solution.py:104
  27.8 4.5 %collective-permute-start.4 = (bf16[1,25,1,512]{3,2,1,0:T(2,128)(2,1)S(1)}, bf16[1,25,1,512]{3,2,1,0:T(2,128)(2,1)S(1)}, u32[]{:S(2)}, u32[]{:S(2)}) collective-permute-start(bf16[1,25,1,512]{3,2,1,0:T(2,128)(2,1)S(1)} %get-tuple-element.35), channel_id=1, source_target_pairs={{0,5},{1,4},{2,7},{3,6},{4,1},{5,0},{6,3},{7,2},{8,13},{9,12},{10,... | collective-permute-start | bytes 76808 | tf_op jit(solution)/shard_map/ppermute | solution.py:104
  29.8 5.2 %collective-permute-start.5 = (bf16[1,25,1,512]{3,2,1,0:T(2,128)(2,1)S(1)}, bf16[1,25,1,512]{3,2,1,0:T(2,128)(2,1)S(1)}, u32[]{:S(2)}, u32[]{:S(2)}) collective-permute-start(bf16[1,25,1,512]{3,2,1,0:T(2,128)(2,1)S(1)} %get-tuple-element.34), channel_id=1, source_target_pairs={{0,6},{1,7},{2,4},{3,5},{4,2},{5,3},{6,0},{7,1},{8,14},{9,15},{10,... | collective-permute-start | bytes 76808 | tf_op jit(solution)/shard_map/ppermute | solution.py:104
  32.0 4.7 %collective-permute-start.6 = (bf16[1,25,1,512]{3,2,1,0:T(2,128)(2,1)S(1)}, bf16[1,25,1,512]{3,2,1,0:T(2,128)(2,1)S(1)}, u32[]{:S(2)}, u32[]{:S(2)}) collective-permute-start(bf16[1,25,1,512]{3,2,1,0:T(2,128)(2,1)S(1)} %get-tuple-element.33), channel_id=1, source_target_pairs={{0,7},{1,6},{2,5},{3,4},{4,3},{5,2},{6,1},{7,0},{8,15},{9,14},{10,... | collective-permute-start | bytes 76808 | tf_op jit(solution)/shard_map/ppermute | solution.py:104
  32.3 6.4 %collective-permute-start.7 = (bf16[1,25,1,512]{3,2,1,0:T(2,128)(2,1)S(1)}, bf16[1,25,1,512]{3,2,1,0:T(2,128)(2,1)S(1)}, u32[]{:S(2)}, u32[]{:S(2)}) collective-permute-start(bf16[1,25,1,512]{3,2,1,0:T(2,128)(2,1)S(1)} %get-tuple-element.32), channel_id=1, source_target_pairs={{0,8},{1,9},{2,10},{3,11},{4,12},{5,13},{6,14},{7,15},{8,0},{9,1},... | collective-permute-start | bytes 76808 | tf_op jit(solution)/shard_map/ppermute | solution.py:104
  35.0 6.2 %collective-permute-start.8 = (bf16[1,25,1,512]{3,2,1,0:T(2,128)(2,1)S(1)}, bf16[1,25,1,512]{3,2,1,0:T(2,128)(2,1)S(1)}, u32[]{:S(2)}, u32[]{:S(2)}) collective-permute-start(bf16[1,25,1,512]{3,2,1,0:T(2,128)(2,1)S(1)} %get-tuple-element.31), channel_id=1, source_target_pairs={{0,9},{1,8},{2,11},{3,10},{4,13},{5,12},{6,15},{7,14},{8,1},{9,0},... | collective-permute-start | bytes 76808 | tf_op jit(solution)/shard_map/ppermute | solution.py:104
  36.7 7.3 %collective-permute-start.9 = (bf16[1,25,1,512]{3,2,1,0:T(2,128)(2,1)S(1)}, bf16[1,25,1,512]{3,2,1,0:T(2,128)(2,1)S(1)}, u32[]{:S(2)}, u32[]{:S(2)}) collective-permute-start(bf16[1,25,1,512]{3,2,1,0:T(2,128)(2,1)S(1)} %get-tuple-element.30), channel_id=1, source_target_pairs={{0,10},{1,11},{2,8},{3,9},{4,14},{5,15},{6,12},{7,13},{8,2},{9,3},... | collective-permute-start | bytes 76808 | tf_op jit(solution)/shard_map/ppermute | solution.py:104
  38.8 7.7 %collective-permute-start.10 = (bf16[1,25,1,512]{3,2,1,0:T(2,128)(2,1)S(1)}, bf16[1,25,1,512]{3,2,1,0:T(2,128)(2,1)S(1)}, u32[]{:S(2)}, u32[]{:S(2)}) collective-permute-start(bf16[1,25,1,512]{3,2,1,0:T(2,128)(2,1)S(1)} %get-tuple-element.29), channel_id=1, source_target_pairs={{0,11},{1,10},{2,9},{3,8},{4,15},{5,14},{6,13},{7,12},{8,3},{9,2},... | collective-permute-start | bytes 76808 | tf_op jit(solution)/shard_map/ppermute | solution.py:104
  41.2 9.0 %collective-permute-start.11 = (bf16[1,25,1,512]{3,2,1,0:T(2,128)(2,1)S(1)}, bf16[1,25,1,512]{3,2,1,0:T(2,128)(2,1)S(1)}, u32[]{:S(2)}, u32[]{:S(2)}) collective-permute-start(bf16[1,25,1,512]{3,2,1,0:T(2,128)(2,1)S(1)} %get-tuple-element.28), channel_id=1, source_target_pairs={{0,12},{1,13},{2,14},{3,15},{4,8},{5,9},{6,10},{7,11},{8,4},{9,5},... | collective-permute-start | bytes 76808 | tf_op jit(solution)/shard_map/ppermute | solution.py:104
  44.0 8.2 %collective-permute-start.12 = (bf16[1,25,1,512]{3,2,1,0:T(2,128)(2,1)S(1)}, bf16[1,25,1,512]{3,2,1,0:T(2,128)(2,1)S(1)}, u32[]{:S(2)}, u32[]{:S(2)}) collective-permute-start(bf16[1,25,1,512]{3,2,1,0:T(2,128)(2,1)S(1)} %get-tuple-element.27), channel_id=1, source_target_pairs={{0,13},{1,12},{2,15},{3,14},{4,9},{5,8},{6,11},{7,10},{8,5},{9,4},... | collective-permute-start | bytes 76808 | tf_op jit(solution)/shard_map/ppermute | solution.py:104
  46.4 7.0 %collective-permute-start.13 = (bf16[1,25,1,512]{3,2,1,0:T(2,128)(2,1)S(1)}, bf16[1,25,1,512]{3,2,1,0:T(2,128)(2,1)S(1)}, u32[]{:S(2)}, u32[]{:S(2)}) collective-permute-start(bf16[1,25,1,512]{3,2,1,0:T(2,128)(2,1)S(1)} %get-tuple-element.41), channel_id=1, source_target_pairs={{0,14},{1,15},{2,12},{3,13},{4,10},{5,11},{6,8},{7,9},{8,6},{9,7},... | collective-permute-start | bytes 76808 | tf_op jit(solution)/shard_map/ppermute | solution.py:104
  50.2 6.4 %collective-permute-start.14 = (bf16[1,25,1,512]{3,2,1,0:T(2,128)(2,1)S(1)}, bf16[1,25,1,512]{3,2,1,0:T(2,128)(2,1)S(1)}, u32[]{:S(2)}, u32[]{:S(2)}) collective-permute-start(bf16[1,25,1,512]{3,2,1,0:T(2,128)(2,1)S(1)} %get-tuple-element.26), channel_id=1, source_target_pairs={{0,15},{1,14},{2,13},{3,12},{4,11},{5,10},{6,9},{7,8},{8,7},{9,6},... | collective-permute-start | bytes 76808 | tf_op jit(solution)/shard_map/ppermute | solution.py:104
  56.8 1.0 copy-start.1
  56.8 1.0 copy-start.4
  56.8 1.0 copy-start.5
  58.1 9.6 %collective-permute-start.19 = (f32[1,10,1,64,128]{4,3,1,2,0:T(8,128)S(1)}, f32[1,10,1,64,128]{4,3,1,2,0:T(8,128)S(1)}, u32[]{:S(2)}, u32[]{:S(2)}) collective-permute-start(f32[1,10,1,64,128]{4,3,1,2,0:T(8,128)S(1)} %get-tuple-element.19), channel_id=1, source_target_pairs={{1,0},{2,1},{3,2},{4,3},{5,4},{6,5},{7,6},{8,7},{9,8},{10,9},{11,1... | collective-permute-start | bytes 983048 | tf_op jit(solution)/shard_map/ppermute | solution.py:21
  59.4 8.3 %collective-permute-start.20 = (f32[1,10,1,64,128]{4,3,1,2,0:T(8,128)S(1)}, f32[1,10,1,64,128]{4,3,1,2,0:T(8,128)S(1)}, u32[]{:S(2)}, u32[]{:S(2)}) collective-permute-start(f32[1,10,1,64,128]{4,3,1,2,0:T(8,128)S(1)} %get-tuple-element.19), channel_id=1, source_target_pairs={{0,1},{1,2},{2,3},{3,4},{4,5},{5,6},{6,7},{7,8},{8,9},{9,10},{10,1... | collective-permute-start | bytes 983048 | tf_op jit(solution)/shard_map/ppermute | solution.py:20
  62.4 3.7 %collective-permute-start.21 = (bf16[1,10,1,1,128]{4,3,1,2,0:T(2,128)(2,1)S(1)}, bf16[1,10,1,1,128]{4,3,1,2,0:T(2,128)(2,1)S(1)}, u32[]{:S(2)}, u32[]{:S(2)}) collective-permute-start(bf16[1,10,1,1,128]{4,3,1,2,0:T(2,128)(2,1)S(1)} %get-tuple-element.76), channel_id=1, source_target_pairs={{0,16},{16,0},{1,17},{17,1},{2,18},{18,2},{3,19},{19,3},{4,20},{20... | collective-permute-start | bytes 7688 | tf_op jit(solution)/shard_map/ppermute | solution.py:20
  63.9 3.6 %collective-permute-start.22 = (bf16[1,10,1,1,128]{4,3,1,2,0:T(2,128)(2,1)S(1)}, bf16[1,10,1,1,128]{4,3,1,2,0:T(2,128)(2,1)S(1)}, u32[]{:S(2)}, u32[]{:S(2)}) collective-permute-start(bf16[1,10,1,1,128]{4,3,1,2,0:T(2,128)(2,1)S(1)} %get-tuple-element.77), channel_id=1, source_target_pairs={{16,0},{0,16},{17,1},{1,17},{18,2},{2,18},{19,3},{3,19},{20,4},{4,... | collective-permute-start | bytes 7688 | tf_op jit(solution)/shard_map/ppermute | solution.py:21
  67.8 0.7 copy-start.6
  68.3 2.6 %copy-start.2 = (f32[1,10,1,64,128]{4,3,1,2,0:T(8,128)}, f32[1,10,1,64,128]{4,3,1,2,0:T(8,128)S(1)}, u32[]{:S(2)}) copy-start(f32[1,10,1,64,128]{4,3,1,2,0:T(8,128)S(1)} %fusion.17) | copy-start | bytes 983044
Sparse Core Ops, SparseCore 0:
  71.0 61.7 reduce-scatter.1
